TPU v7x, 32 devices: a whole 2x2x4 slice. The times are simulated.
32 devices in a mesh: stn: 8 (over z, core), win: 4 (over y, x).
Axes of the slice: x: 2, y: 2, z: 4, core: 2. Of those that a mesh axis runs over, the one named last changes fastest.
Arguments:
- records: bfloat16 [128, 4, 3, 8192], P('stn', 'win'), may hold values from -6 to 6
- observed: float32 [128, 3, 3, 256], P('stn'), may hold values from -6 to 6
- lag_lo: int32 [128], P('stn'), may hold values from 0 to 63
- lag_hi: int32 [128], P('stn'), may hold values from 192 to 256
- send_table: int32 [8, 8, 1], P('stn'), may hold values from 0 to 15, as said below
- pair_first: int32 [128], P('stn'), may hold values from 0 to 7, as said below
- pair_second: int32 [128], P('stn'), may hold values from 0 to 7, as said below
Outputs:
- station_adjoint: bfloat16 [128, 4, 3, 8192], P('stn', 'win')
- residual: float32 [128, 3, 3, 256], P(('stn', 'win'))
Inputs may be any that keep to these rules, and one draw needn't show every extreme that they name: Each entry send_table[g, o, :] names 1 different local stations of group g. `pair_first`: slot indices at the pair's owner; a pair's two slots differ, no two pairs of an owner join the same two slots, and every slot of an owner is named by some pair. `pair_second`: slot indices at the pair's owner, as for pair_first.
All inputs are finite; a program needn't handle non-finite values.
Results may differ from a plain program's by a relative error of at most 0.0053.
Values may be sent and summed in bfloat16 or wider, within the bound.
No kernel may reach another device: no remote copies, remote signals or barrier semaphores. Data moves between devices by JAX's collectives and lax.ppermute only.
A program may use at most 192 MiB of HBM per device.

v0:
```python
import math
import jax
import jax.numpy as jnp
from jax import lax
from jax.sharding import PartitionSpec as P

LAGS = 256


def forward_table(lag_count):
    period = 2 * lag_count
    sample_ids = jnp.arange(lag_count, dtype=jnp.int32)
    freq_ids = jnp.arange(lag_count, dtype=jnp.int32)
    phase = (sample_ids[:, None] * freq_ids[None, :] % period).astype(jnp.float32) * (
        math.pi / lag_count
    )
    parity = (1 - 2 * (sample_ids % 2)).astype(jnp.float32)
    cosines = jnp.cos(phase)
    sines = jnp.where(freq_ids[None, :] == 0, parity[:, None], jnp.sin(phase))
    return jnp.concatenate([cosines, sines], axis=1)


def inverse_rows(positions, sine_sign, lag_count):
    period = 2 * lag_count
    freq_ids = jnp.arange(lag_count, dtype=jnp.int32)
    wrapped = positions % period
    phase = (freq_ids[:, None] * wrapped[None, :] % period).astype(jnp.float32) * (
        math.pi / lag_count
    )
    weight = jnp.where(freq_ids == 0, 1.0 / period, 2.0 / period).astype(jnp.float32)
    cos_rows = weight[:, None] * jnp.cos(phase)
    parity = (1 - 2 * (wrapped % 2)).astype(jnp.float32) / period
    sin_rows = jnp.where(
        freq_ids[:, None] == 0, parity[None, :], sine_sign * (2.0 / period) * jnp.sin(phase)
    )
    return jnp.concatenate([cos_rows, sin_rows], axis=0)


def shards(records, observed, lag_lo, lag_hi, send_table, pair_first, pair_second):
    owner_count = lax.axis_size("stn")
    window_groups = lax.axis_size("win")
    send_rows = send_table[0]
    cap_count = send_rows.shape[1]
    slot_count = owner_count * cap_count
    local_windows = records.shape[1]
    samples = records.shape[3]
    station_count = records.shape[0]
    lag_count = LAGS
    half_lag = lag_count // 2
    block_total = samples // lag_count
    highest = lax.Precision.HIGHEST
    outgoing = jnp.take(records, send_rows.reshape(-1), axis=0)
    outgoing = outgoing.reshape((owner_count, cap_count) + records.shape[1:])
    arrived = lax.all_to_all(outgoing, "stn", split_axis=0, concat_axis=0, tiled=True)
    slot_records = arrived.reshape((slot_count,) + records.shape[1:])
    spectral = forward_table(lag_count)
    lag_ids = jnp.arange(lag_count, dtype=jnp.int32)
    corr_table = inverse_rows(lag_ids, -1.0, lag_count)
    middle_table = inverse_rows(lag_ids + half_lag, 1.0, lag_count)
    lower_table = (
        inverse_rows(lag_ids + 3 * half_lag, 1.0, lag_count)
        * (lag_ids < half_lag).astype(jnp.float32)[None, :]
    )
    upper_table = (
        inverse_rows(lag_ids - half_lag, 1.0, lag_count)
        * (lag_ids >= half_lag).astype(jnp.float32)[None, :]
    )
    column_ids = jnp.arange(2 * lag_count, dtype=jnp.int32)
    shift_sign = (1 - 2 * (column_ids % lag_count % 2)).astype(jnp.float32)
    first_col = (lag_ids == 0).astype(jnp.float32)
    other_cols = 1.0 - first_col
    block_shape = (slot_count, local_windows, 3, block_total, lag_count)
    first_blocks = slot_records.astype(jnp.float32).reshape(block_shape)
    x_spec = jnp.dot(first_blocks, spectral, precision=highest)
    shifted = jnp.pad(slot_records, ((0, 0), (0, 0), (0, 0), (half_lag, lag_count - half_lag)))
    shifted = shifted.astype(jnp.float32).reshape(
        (slot_count, local_windows, 3, block_total + 1, lag_count)
    )
    z_spec = jnp.dot(shifted, spectral, precision=highest)
    y_spec = z_spec[..., :-1, :] + shift_sign * z_spec[..., 1:, :]
    slot_ids = jnp.arange(slot_count, dtype=jnp.int32)
    first_hot = (pair_first[:, None] == slot_ids[None, :]).astype(jnp.float32)
    second_hot = (pair_second[:, None] == slot_ids[None, :]).astype(jnp.float32)
    x_pair = jnp.einsum("ps,swakf->pwakf", first_hot, x_spec, precision=highest)
    y_pair = jnp.einsum("ps,swakf->pwakf", second_hot, y_spec, precision=highest)
    x_cos = x_pair[..., :lag_count]
    x_sin = x_pair[..., lag_count:]
    y_cos = y_pair[..., :lag_count]
    y_sin = y_pair[..., lag_count:]
    y_sin_other = y_sin * other_cols
    y_mixed = y_sin * first_col + y_cos * other_cols

    def cross_terms(left, right):
        return jnp.einsum("pwakf,pwbkf->pabf", left, right, precision=highest)

    real_part = cross_terms(x_cos, y_cos) + cross_terms(x_sin, y_sin_other)
    imag_part = cross_terms(x_sin, y_mixed) - cross_terms(x_cos, y_sin_other)
    cross = jnp.concatenate([real_part, imag_part], axis=-1)
    partial_corr = jnp.dot(cross, corr_table, precision=highest)
    pair_count = partial_corr.shape[0]
    corr_scale = 1.0 / math.sqrt(samples * local_windows * window_groups)
    lag_mask = (lag_ids[None, :] >= lag_lo[:, None]) & (lag_ids[None, :] < lag_hi[:, None])
    share_rows = pair_count // window_groups
    offset = lax.axis_index("win") * share_rows
    summed = lax.psum(partial_corr, "win")
    residual_all = jnp.where(lag_mask[:, None, None, :], summed * corr_scale - observed, 0.0)
    adjoint_source = residual_all.astype(jnp.bfloat16)
    residual_share = lax.dynamic_slice_in_dim(residual_all, offset, share_rows, 0)
    source_spec = jnp.dot(adjoint_source.astype(jnp.float32), spectral, precision=highest)
    src_cos = source_spec[..., :lag_count]
    src_sin = source_spec[..., lag_count:]
    src_cos_other = src_cos * other_cols
    src_sin_other = src_sin * other_cols
    src_sin_first = src_sin * first_col

    def first_terms(source, data):
        return jnp.einsum("pabf,pwbkf->pwakf", source, data, precision=highest)

    first_real = first_terms(src_cos, y_cos) + first_terms(src_sin_other, y_sin)
    first_imag = first_terms(src_sin, y_mixed) - first_terms(src_cos_other, y_sin)
    first_pair = jnp.concatenate([first_real, first_imag], axis=-1)
    first_acc = jnp.einsum("ps,pwakf->swakf", first_hot, first_pair, precision=highest)

    def second_terms(data, source):
        return jnp.einsum("pwakf,pabf->pwbkf", data, source, precision=highest)

    second_real = second_terms(x_cos, src_cos) - second_terms(x_sin, src_sin_other)
    second_imag = (
        second_terms(x_cos, src_sin_other)
        + second_terms(x_sin, src_cos_other)
        + second_terms(x_sin, src_sin_first)
    )
    second_pair = jnp.concatenate([second_real, second_imag], axis=-1)
    second_acc = jnp.einsum("ps,pwakf->swakf", second_hot, second_pair, precision=highest)
    first_time = jnp.dot(first_acc, corr_table, precision=highest)
    middle = jnp.dot(second_acc, middle_table, precision=highest)
    from_lower = jnp.dot(second_acc, lower_table, precision=highest)
    from_upper = jnp.dot(second_acc, upper_table, precision=highest)
    spacer = ((0, 0), (0, 0), (0, 0))
    from_lower = jnp.pad(from_lower[..., :-1, :], spacer + ((1, 0), (0, 0)))
    from_upper = jnp.pad(from_upper[..., 1:, :], spacer + ((0, 1), (0, 0)))
    slot_sum = (first_time + middle + from_lower + from_upper).reshape(
        (slot_count,) + records.shape[1:]
    )
    adj_scale = 1.0 / math.sqrt(3 * lag_count)
    slot_adjoint = (slot_sum * adj_scale).astype(jnp.bfloat16)
    slot_adjoint = slot_adjoint.reshape((owner_count, cap_count) + records.shape[1:])
    station_ids = jnp.arange(station_count, dtype=jnp.int32)
    station_hot = (send_rows.reshape(-1)[None, :] == station_ids[:, None]).astype(jnp.bfloat16)
    returned = lax.all_to_all(slot_adjoint, "stn", split_axis=0, concat_axis=0, tiled=True)
    flat_rows = returned.reshape((slot_count, -1))
    totals = jnp.dot(station_hot, flat_rows, preferred_element_type=jnp.float32)
    station_adjoint = totals.reshape((station_count,) + returned.shape[2:]).astype(jnp.bfloat16)
    return (station_adjoint, residual_share)


def solution(mesh):
    placed = (
        P("stn", "win", None, None),
        P("stn", None, None, None),
        P("stn"),
        P("stn"),
        P("stn", None, None),
        P("stn"),
        P("stn"),
    )
    return jax.shard_map(
        shards,
        mesh=mesh,
        in_specs=placed,
        out_specs=(P("stn", "win", None, None), P(("stn", "win"), None, None, None)),
        check_vma=False,
    )
```

profile of v0, /device:TPU:0, one launch (start us, length us, event | category | flops | bytes accessed | tf_op | source)
XLA Modules:
  0.0 665.9 jit_solution(7594870986401893331)
XLA Ops:
  12.4 6.3 all-to-all-start
  20.7 6.3 cosine_multiply_fusion.2
  27.0 7.1 %all-to-all-done = bf16[8,1,1,3,8192]{4,3,2,1,0:T(4,128)(2,1)S(1)} async-done(((bf16[8,1,1,3,8192]{4,3,2,1,0:T(4,128)(2,1)}), bf16[8,1,1,3,8192]{4,3,2,1,0:T(4,128)(2,1)S(1)}, u32[]{:S(2)}, u32[]{:S(2)}) %all-to-all-start) | async-done | bytes 393248 | tf_op jit(solution)/shard_map/all_to_all | solution.py:54
  41.2 6.1 copy.158
  52.3 6.2 copy.157
  58.5 6.1 copy.156
  64.6 6.1 copy.155
  70.7 30.7 %fusion.150 = f32[16,256,3,3]{3,2,1,0:T(4,128)S(1)} fusion(f32[16,3,32,256]{2,1,3,0:T(4,128)} %copy.158, f32[16,3,32,256]{2,1,3,0:T(4,128)} %copy.157), kind=kOutput, calls=%fused_computation.225 | convolution fusion | flops 14155776 | bytes 3293184 | tf_op jit(solution)/shard_map/pwakf,pwbkf->pabf/dot_general | solution.py:94
  101.4 29.8 %subtract_bitcast_fusion.2 = f32[16,3,3,256]{1,2,3,0:T(4,128)} fusion(f32[16,256,3,3]{3,2,1,0:T(4,128)S(1)} %fusion.150, f32[16,3,32,256]{2,1,3,0:T(4,128)S(1)} %copy-done.1, f32[16,3,32,256]{2,1,3,0:T(4,128)S(1)} %copy-done), kind=kOutput, calls=%fused_computation.9 | convolution fusion | flops 14192640 | bytes 3440640 | tf_op jit(solution)/shard_map/pwakf,pwbkf->pabf/dot_general | solution.py:94
  131.2 4.9 copy.163
  136.2 6.1 copy.164
  142.3 30.4 %fusion.149 = f32[16,256,3,3]{3,2,1,0:T(4,128)S(1)} fusion(f32[16,3,32,256]{2,1,3,0:T(4,128)} %copy.164, f32[16,3,32,256]{2,1,3,0:T(4,128)} %copy.155), kind=kOutput, calls=%fused_computation.224 | convolution fusion | flops 14155776 | bytes 3293184 | tf_op jit(solution)/shard_map/pwakf,pwbkf->pabf/dot_general | solution.py:94
  172.7 31.9 %add_bitcast_fusion.2 = f32[16,3,3,256]{1,2,3,0:T(4,128)} fusion(f32[16,256,3,3]{3,2,1,0:T(4,128)S(1)} %fusion.149, f32[16,3,32,256]{2,1,3,0:T(4,128)} %copy.156, f32[16,3,32,256]{2,1,3,0:T(4,128)} %copy.157), kind=kOutput, calls=%fused_computation.10 | convolution fusion | flops 14192640 | bytes 3440640 | tf_op jit(solution)/shard_map/pwakf,pwbkf->pabf/dot_general | solution.py:94
  204.6 5.0 copy.162
  211.8 4.7 copy.166
  216.6 35.3 %all-reduce.5.cloned.1.call-done = f32[16,3,3,256]{3,0,2,1:T(8,128)} async-done(((f32[16,3,3,256]{3,0,2,1:T(8,128)}), f32[16,3,3,256]{3,0,2,1:T(8,128)}) %all-reduce.5.cloned.1.call-update) | async-done | bytes 147472 | tf_op jit(solution)/shard_map/psum | solution.py:105
  253.5 4.7 copy.174
  258.2 37.4 %fusion.151 = f32[16,256,32,3]{2,3,1,0:T(4,128)} fusion(f32[16,3,32,256]{2,1,3,0:T(4,128)} %copy.164, f32[16,3,3,256]{1,2,3,0:T(4,128)} %copy.174), kind=kOutput, calls=%fused_computation.226 | convolution fusion | flops 14155776 | bytes 3293184 | tf_op jit(solution)/shard_map/pabf,pwbkf->pwakf/dot_general | solution.py:117
  295.6 30.2 %fusion.153 = f32[16,256,3,32]{3,2,1,0:T(4,128)} fusion(f32[16,3,3,256]{1,2,3,0:T(4,128)S(1)} %copy-done.3, f32[16,3,32,256]{2,1,3,0:T(4,128)} %copy.155), kind=kOutput, calls=%fused_computation.228 | convolution fusion | flops 14155776 | bytes 3293184 | tf_op jit(solution)/shard_map/pwakf,pabf->pwbkf/dot_general | solution.py:125
  330.4 32.4 %fusion.152 = f32[16,256,32,3]{2,3,1,0:T(4,128)} fusion(f32[16,3,32,256]{2,1,3,0:T(4,128)} %copy.158, f32[16,3,3,256]{2,1,3,0:T(4,128)} %copy.169), kind=kOutput, calls=%fused_computation.227 | convolution fusion | flops 14155776 | bytes 3293184 | tf_op jit(solution)/shard_map/pabf,pwbkf->pwakf/dot_general | solution.py:117
  362.8 4.7 copy.180
  372.1 31.0 %fusion.154 = f32[16,256,3,32]{3,2,1,0:T(4,128)} fusion(f32[16,3,3,256]{1,2,3,0:T(4,128)} %copy.176, f32[16,3,32,256]{2,1,3,0:T(4,128)} %copy.155), kind=kOutput, calls=%fused_computation.229 | convolution fusion | flops 14155776 | bytes 3293184 | tf_op jit(solution)/shard_map/pwakf,pabf->pwbkf/dot_general | solution.py:125
  403.1 30.8 %fusion.155 = f32[16,256,3,32]{3,2,1,0:T(4,128)} fusion(f32[16,3,3,256]{1,2,3,0:T(4,128)S(1)} %copy-done.2, f32[16,3,32,256]{2,1,3,0:T(4,128)} %copy.157), kind=kOutput, calls=%fused_computation.230 | convolution fusion | flops 14155776 | bytes 3293184 | tf_op jit(solution)/shard_map/pwakf,pabf->pwbkf/dot_general | solution.py:125
  433.9 36.6 %subtract_bitcast_fusion.1 = f32[16,1,3,32,256]{3,2,4,0,1:T(4,128)} fusion(f32[16,256,32,3]{2,3,1,0:T(4,128)} %fusion.152, f32[16,3,32,256]{2,1,3,0:T(4,128)S(1)} %bitcast.169, f32[16,3,3,256]{1,2,3,0:T(4,128)S(1)} %copy-done.2), kind=kOutput, calls=%fused_computation.7 | convolution fusion | flops 14548992 | bytes 4866048 | tf_op jit(solution)/shard_map/pabf,pwbkf->pwakf/dot_general | solution.py:117
  470.6 36.0 %add_bitcast_fusion.1 = f32[16,1,3,32,256]{3,2,4,0,1:T(4,128)} fusion(f32[16,256,32,3]{2,3,1,0:T(4,128)S(1)} %bitcast.171, f32[16,3,32,256]{2,1,3,0:T(4,128)S(1)} %bitcast.169, f32[16,3,3,256]{1,2,3,0:T(4,128)S(1)} %bitcast.167), kind=kOutput, calls=%fused_computation.8 | convolution fusion | flops 14548992 | bytes 4866048 | tf_op jit(solution)/shard_map/pabf,pwbkf->pwakf/dot_general | solution.py:117
  506.5 12.0 %maximum_bitcast_fusion = f32[16,3,32,512]{2,1,3,0:T(4,128)} fusion(f32[16,1,3,32,256]{3,2,4,0,1:T(4,128)S(1)} %copy-done.5, f32[16,1,3,32,256]{3,2,4,0,1:T(4,128)} %add_bitcast_fusion.1), kind=kLoop, calls=%fused_computation.1 | loop fusion | flops 786432 | bytes 6291456 | tf_op jit(solution)/shard_map/reshape.43
  518.5 9.5 %copy.172 = f32[16,3,32,512]{3,0,2,1:T(8,128)S(1)} copy(f32[16,3,32,512]{2,1,3,0:T(4,128)} %maximum_bitcast_fusion) | data formatting | bytes 6291456 | tf_op jit(solution)/shard_map/reshape.43
  538.6 31.8 %subtract_bitcast_fusion = f32[16,1,3,32,256]{3,2,4,0,1:T(4,128)} fusion(f32[16,256,3,32]{3,2,1,0:T(4,128)} %fusion.153, f32[16,3,3,256]{1,2,3,0:T(4,128)} %copy.176, f32[16,3,32,256]{2,1,3,0:T(4,128)} %copy.157), kind=kOutput, calls=%fused_computation.6 | convolution fusion | flops 14548992 | bytes 4866048 | tf_op jit(solution)/shard_map/pwakf,pabf->pwbkf/dot_general | solution.py:125
  570.4 31.8 %add_bitcast_fusion = f32[16,1,3,32,256]{3,2,4,0,1:T(4,128)} fusion(f32[16,256,3,32]{3,2,1,0:T(4,128)} %fusion.154, f32[16,256,3,32]{3,2,1,0:T(4,128)} %fusion.155, f32[16,3,3,256]{1,2,3,0:T(4,128)S(1)} %copy-done.4, f32[16,3,32,256]{2,1,3,0:T(4,128)} %copy.157), kind=kOutput, calls=%fused_computation.5 | convolution fusion | flops 14942208 | bytes 6438912 | tf_op jit(solution)/shard_map/pwakf,pabf->pwbkf/dot_general | solution.py:125
  602.2 15.0 %maximum_bitcast_fusion.1 = f32[16,3,32,512]{2,1,3,0:T(4,128)} fusion(f32[16,1,3,32,256]{3,2,4,0,1:T(4,128)} %add_bitcast_fusion, f32[16,1,3,32,256]{3,2,4,0,1:T(4,128)} %subtract_bitcast_fusion), kind=kLoop, calls=%fused_computation.2 | loop fusion | flops 786432 | bytes 6291456 | tf_op jit(solution)/shard_map/reshape.57
  617.2 9.8 %copy.184 = f32[16,3,32,512]{3,0,2,1:T(8,128)S(1)} copy(f32[16,3,32,512]{2,1,3,0:T(4,128)} %maximum_bitcast_fusion.1) | data formatting | bytes 6291456 | tf_op jit(solution)/shard_map/reshape.57
  643.2 13.9 %all-to-all-done.1 = bf16[8,1,1,3,8192]{4,3,2,1,0:T(4,128)(2,1)S(1)} async-done(((bf16[8,1,1,3,8192]{4,3,2,1,0:T(4,128)(2,1)}), bf16[8,1,1,3,8192]{4,3,2,1,0:T(4,128)(2,1)S(1)}, u32[]{:S(2)}, u32[]{:S(2)}) %all-to-all-start.1) | async-done | bytes 393248 | tf_op jit(solution)/shard_map/all_to_all | solution.py:150
  (119 shorter events, 60.2 us)
Async XLA Ops:
  8.5 27.6 %copy-start.22 = (s32[16]{0:T(128)S(1)}, s32[16]{0:T(128)}, u32[]{:S(2)}) copy-start(s32[16]{0:T(128)} %param.13) | copy-start | bytes 196
  12.4 21.7 %all-to-all-start = ((bf16[8,1,1,3,8192]{4,3,2,1,0:T(4,128)(2,1)}), bf16[8,1,1,3,8192]{4,3,2,1,0:T(4,128)(2,1)S(1)}, u32[]{:S(2)}, u32[]{:S(2)}) async-start(bf16[8,1,1,3,8192]{4,3,2,1,0:T(4,128)(2,1)} %fusion.46), calls=%async_computation | async-start | bytes 1048576 | tf_op jit(solution)/shard_map/all_to_all | solution.py:54
  18.7 233.2 %all-reduce.5.cloned.1.call-start = ((), (), s32[]{:S(2)}) async-start(), calls=%async_computation.2 | async-start | bytes 294912 | tf_op jit(solution)/shard_map/psum | solution.py:105
  18.9 19.3 %copy-start.17 = (f32[256]{0:T(256)}, f32[256]{0:T(256)S(1)}, u32[]{:S(2)}) copy-start(f32[256]{0:T(256)S(1)} %broadcast_subtract_fusion) | copy-start | bytes 3076
  18.9 19.3 %copy-start.19 = (f32[256]{0:T(256)}, f32[256]{0:T(256)S(1)}, u32[]{:S(2)}) copy-start(f32[256]{0:T(256)S(1)} %fusion.138) | copy-start | bytes 3076
  41.2 7.6 %copy-start.21 = (s32[16]{0:T(128)S(1)}, s32[16]{0:T(128)}, u32[]{:S(2)}) copy-start(s32[16]{0:T(128)} %param.12) | copy-start | bytes 196
  70.7 30.7 %copy-start = (f32[16,3,32,256]{2,1,3,0:T(4,128)S(1)}, f32[16,3,32,256]{2,1,3,0:T(4,128)}, u32[]{:S(2)}) copy-start(f32[16,3,32,256]{2,1,3,0:T(4,128)} %copy.155) | copy-start | bytes 4718596
  70.7 30.7 %copy-start.1 = (f32[16,3,32,256]{2,1,3,0:T(4,128)S(1)}, f32[16,3,32,256]{2,1,3,0:T(4,128)}, u32[]{:S(2)}) copy-start(f32[16,3,32,256]{2,1,3,0:T(4,128)} %copy.156) | copy-start | bytes 4718596
  204.6 5.0 copy-start.7
  204.6 5.0 copy-start.9
  204.6 47.3 %copy-start.16 = (f32[16,3,3,256]{3,0,2,1:T(8,128)S(1)}, f32[16,3,3,256]{3,0,2,1:T(8,128)}, u32[]{:S(2)}) copy-start(f32[16,3,3,256]{3,0,2,1:T(8,128)} %param.8) | copy-start | bytes 442372
  204.6 48.6 %copy-start.18 = (f32[256]{0:T(256)S(1)}, f32[256]{0:T(256)}, u32[]{:S(2)}) copy-start(f32[256]{0:T(256)} %copy-done.17) | copy-start | bytes 3076
  204.6 48.6 %copy-start.20 = (f32[256]{0:T(256)S(1)}, f32[256]{0:T(256)}, u32[]{:S(2)}) copy-start(f32[256]{0:T(256)} %copy-done.19) | copy-start | bytes 3076
  258.2 37.4 %copy-start.3 = (f32[16,3,3,256]{1,2,3,0:T(4,128)S(1)}, f32[16,3,3,256]{1,2,3,0:T(4,128)}, u32[]{:S(2)}) copy-start(f32[16,3,3,256]{1,2,3,0:T(4,128)} %copy.174) | copy-start | bytes 442372
  372.1 31.0 %copy-start.2 = (f32[16,3,3,256]{1,2,3,0:T(4,128)S(1)}, f32[16,3,3,256]{1,2,3,0:T(4,128)}, u32[]{:S(2)}) copy-start(f32[16,3,3,256]{1,2,3,0:T(4,128)} %copy.180) | copy-start | bytes 442372
  372.1 61.8 %slice-start.2 = ((s8[8388608]{0:T(1024)(128)(4,1)}), s8[4194304]{0:T(1024)(128)(4,1)S(1)}, s32[]{:S(2)}) async-start(s8[8388608]{0:T(1024)(128)(4,1)} %bitcast.168), calls=%async_computation.5 | async-start | bytes 8388608
  403.1 30.8 %slice-start.3 = ((s8[8388608]{0:T(1024)(128)(4,1)}), s8[4194304]{0:T(1024)(128)(4,1)S(1)}, s32[]{:S(2)}) async-start(s8[8388608]{0:T(1024)(128)(4,1)} %bitcast.168), calls=%async_computation.6 | async-start | bytes 8388608
  403.1 67.5 %slice-start = ((s8[8388608]{0:T(1024)(128)(4,1)}), s8[4194304]{0:T(1024)(128)(4,1)S(1)}, s32[]{:S(2)}) async-start(s8[8388608]{0:T(1024)(128)(4,1)} %bitcast.166), calls=%async_computation.3 | async-start | bytes 8388608
  403.1 67.5 %slice-start.4 = ((s8[8388608]{0:T(1024)(128)(4,1)}), s8[4194304]{0:T(1024)(128)(4,1)S(1)}, s32[]{:S(2)}) async-start(s8[8388608]{0:T(1024)(128)(4,1)} %bitcast.170), calls=%async_computation.7 | async-start | bytes 8388608
  433.9 36.6 %slice-start.1 = ((s8[8388608]{0:T(1024)(128)(4,1)}), s8[4194304]{0:T(1024)(128)(4,1)S(1)}, s32[]{:S(2)}) async-start(s8[8388608]{0:T(1024)(128)(4,1)} %bitcast.166), calls=%async_computation.4 | async-start | bytes 8388608
  433.9 36.6 %slice-start.5 = ((s8[8388608]{0:T(1024)(128)(4,1)}), s8[4194304]{0:T(1024)(128)(4,1)S(1)}, s32[]{:S(2)}) async-start(s8[8388608]{0:T(1024)(128)(4,1)} %bitcast.170), calls=%async_computation.8 | async-start | bytes 8388608
  470.6 36.0 %copy-start.5 = (f32[16,1,3,32,256]{3,2,4,0,1:T(4,128)S(1)}, f32[16,1,3,32,256]{3,2,4,0,1:T(4,128)}, u32[]{:S(2)}) copy-start(f32[16,1,3,32,256]{3,2,4,0,1:T(4,128)} %subtract_bitcast_fusion.1) | copy-start | bytes 4718596
  518.5 11.4 %copy-start.8 = (f32[256,256]{1,0:T(8,128)S(1)}, f32[256,256]{1,0:T(8,128)}, u32[]{:S(2)}) copy-start(f32[256,256]{1,0:T(8,128)} %get-tuple-element.19) | copy-start | bytes 786436
  538.6 31.8 %copy-start.4 = (f32[16,3,3,256]{1,2,3,0:T(4,128)S(1)}, f32[16,3,3,256]{1,2,3,0:T(4,128)}, u32[]{:S(2)}) copy-start(f32[16,3,3,256]{1,2,3,0:T(4,128)} %copy.182) | copy-start | bytes 442372
  617.2 9.8 %copy-start.23 = (s32[16]{0:T(128)S(1)}, s32[16]{0:T(128)}, u32[]{:S(2)}) copy-start(s32[16]{0:T(128)} %param.13) | copy-start | bytes 196
  617.2 11.1 %copy-start.14 = (f32[256,256]{1,0:T(8,128)S(1)}, f32[256,256]{1,0:T(8,128)}, u32[]{:S(2)}) copy-start(f32[256,256]{1,0:T(8,128)} %get-tuple-element.17) | copy-start | bytes 786436
  617.2 11.1 %copy-start.25 = (f32[256]{0:T(256)S(1)}, f32[256]{0:T(256)}, u32[]{:S(2)}) copy-start(f32[256]{0:T(256)} %compare_convert_fusion) | copy-start | bytes 3076
  627.0 6.7 %copy-start.6 = (f32[8,3,32,256]{3,2,1,0:T(8,128)S(1)}, f32[8,3,32,256]{3,2,1,0:T(8,128)}, u32[]{:S(2)}) copy-start(f32[8,3,32,256]{3,2,1,0:T(8,128)} %fusion.3) | copy-start | bytes 2359300
  627.1 6.7 %copy-start.10 = (f32[256,256]{1,0:T(8,128)S(1)}, f32[256,256]{1,0:T(8,128)}, u32[]{:S(2)}) copy-start(f32[256,256]{1,0:T(8,128)} %get-tuple-element.13) | copy-start | bytes 786436
  627.1 6.7 %copy-start.11 = (f32[256,256]{1,0:T(8,128)S(1)}, f32[256,256]{1,0:T(8,128)}, u32[]{:S(2)}) copy-start(f32[256,256]{1,0:T(8,128)} %get-tuple-element.14) | copy-start | bytes 786436
  627.1 29.9 %copy-start.26 = (s32[1,8,1]{1,2,0:T(1,128)S(1)}, s32[1,8,1]{1,2,0:T(1,128)}, u32[]{:S(2)}) copy-start(s32[1,8,1]{1,2,0:T(1,128)} %param.11) | copy-start | bytes 100
  637.0 20.0 %all-to-all-start.1 = ((bf16[8,1,1,3,8192]{4,3,2,1,0:T(4,128)(2,1)}), bf16[8,1,1,3,8192]{4,3,2,1,0:T(4,128)(2,1)S(1)}, u32[]{:S(2)}, u32[]{:S(2)}) async-start(bf16[8,1,1,3,8192]{4,3,2,1,0:T(4,128)(2,1)} %bitcast.61), calls=%async_computation.1 | async-start | bytes 1048576 | tf_op jit(solution)/shard_map/all_to_all | solution.py:150
  (4 other events, 14.2 us)
Sparse Core Ops, SparseCore 0:
  210.9 41.0 all-reduce.4
where the time goes:
time: 670 us; the launch traced here: 666 us
  matrix products  444 us (66%)
  local copies, waits for them, and re-layouts  96.7 us (14%)
  waiting for transfers between devices  56.3 us (8%)
  other arithmetic  42.8 us (6%)
  between operations  15.1 us (2%)
  starting transfers between devices  11 us (2%)
    dot_general x5, matrix products, second_terms(): return jnp.einsum('pwakf,pabf->pwbkf', data, source, precision=highest)  156 us
    dot_general x4, matrix products, first_terms(): return jnp.einsum('pabf,pwbkf->pwakf', source, data, precision=highest)  142 us
    dot_general x4, matrix products, cross_terms(): return jnp.einsum('pwakf,pwbkf->pabf', left, right, precision=highest)  123 us
    another operation x11, local copies, waits for them, and re-layouts  57.7 us
    psum x1, waiting for transfers between devices, shards(): summed = lax.psum(partial_corr, 'win')  35.3 us
    another operation x4, other arithmetic  30.2 us
    all_to_all x1, waiting for transfers between devices, shards(): lax.all_to_all(slot_adjoint, 'stn', split_axis=0, concat_axis=0, tiled=True)  13.9 us
  transfers between devices with their start and end apart: 3, of which 3 were waited for; matrix products, arithmetic and copies ran while one was open for 2% of the time, Pallas kernels for 0%

commit v1 on v0

--- a/solution.py
+++ b/solution.py
@@ -5,6 +5,11 @@
 from jax.sharding import PartitionSpec as P
 
 LAGS = 256
+
+
+def gather_and_add(block, mesh_axis):
+    parts = lax.all_gather(block, mesh_axis)
+    return jnp.sum(parts, axis=0)
 
 
 def forward_table(lag_count):
@@ -102,7 +107,7 @@
     lag_mask = (lag_ids[None, :] >= lag_lo[:, None]) & (lag_ids[None, :] < lag_hi[:, None])
     share_rows = pair_count // window_groups
     offset = lax.axis_index("win") * share_rows
-    summed = lax.psum(partial_corr, "win")
+    summed = gather_and_add(partial_corr, "win")
     residual_all = jnp.where(lag_mask[:, None, None, :], summed * corr_scale - observed, 0.0)
     adjoint_source = residual_all.astype(jnp.bfloat16)
     residual_share = lax.dynamic_slice_in_dim(residual_all, offset, share_rows, 0)

time: 670 us -> 634 us (0.946)
  waiting for transfers between devices: 56.3 us -> 19.9 us
  between operations: 15.1 us -> 1.73 us
  blocking collectives: 0 us -> 10.3 us
    psum x1 -> x0, waiting for transfers between devices: 35.3 us -> none  [shards(): summed = lax.psum(partial_corr, 'win')]
    all_gather x0 -> x1, blocking collectives: none -> 10.3 us  [gather_and_add(): parts = lax.all_gather(block, mesh_axis)]
  transfers between devices with their start and end apart: 3 -> 2, of which waited for: 3 -> 2; matrix products, arithmetic and copies ran while one was open for 2% -> 2% of each run, Pallas kernels for 0% -> 0%
where the time goes in v1:
time: 634 us; the launch traced here: 624 us
  matrix products  443 us (70%)
  local copies, waits for them, and re-layouts  97.7 us (15%)
  other arithmetic  41.7 us (7%)
  waiting for transfers between devices  19.9 us (3%)
  blocking collectives  10.3 us (2%)
  starting transfers between devices  9.82 us (2%)
    dot_general x5, matrix products, second_terms(): return jnp.einsum('pwakf,pabf->pwbkf', data, source, precision=highest)  156 us
    dot_general x4, matrix products, first_terms(): return jnp.einsum('pabf,pwbkf->pwakf', source, data, precision=highest)  142 us
    dot_general x4, matrix products, cross_terms(): return jnp.einsum('pwakf,pwbkf->pabf', left, right, precision=highest)  123 us
    another operation x11, local copies, waits for them, and re-layouts  58 us
    another operation x4, other arithmetic  30.1 us
    all_to_all x1, waiting for transfers between devices, shards(): lax.all_to_all(slot_adjoint, 'stn', split_axis=0, concat_axis=0, tiled=True)  13.8 us
  transfers between devices with their start and end apart: 2, of which 2 were waited for; matrix products, arithmetic and copies ran while one was open for 2% of the time, Pallas kernels for 0%

profile of v1, /device:TPU:0, one launch (start us, length us, event | category | flops | bytes accessed | tf_op | source)
XLA Modules:
  0.0 623.9 jit_solution(2103884950038483247)
XLA Ops:
  5.9 6.3 %all-to-all-start = ((bf16[8,1,1,3,8192]{4,3,2,1,0:T(4,128)(2,1)}), bf16[8,1,1,3,8192]{4,3,2,1,0:T(4,128)(2,1)S(1)}, u32[]{:S(2)}, u32[]{:S(2)}) async-start(bf16[8,1,1,3,8192]{4,3,2,1,0:T(4,128)(2,1)} %fusion.46), calls=%async_computation | async-start | bytes 1048576 | tf_op jit(solution)/shard_map/all_to_all | solution.py:59
  15.2 6.1 cosine_multiply_fusion.2
  21.4 6.2 all-to-all-done
  34.6 6.2 copy.158
  45.8 6.2 copy.157
  52.0 6.3 %copy.156 = f32[16,3,32,256]{2,1,3,0:T(4,128)} copy(f32[16,3,32,256]{3,0,2,1:T(8,128)} %get-tuple-element.2) | data formatting | bytes 3145728 | tf_op jit(solution)/shard_map/reshape.27
  58.2 6.1 copy.155
  64.4 30.4 %fusion.150 = f32[16,256,3,3]{3,2,1,0:T(4,128)S(1)} fusion(f32[16,3,32,256]{2,1,3,0:T(4,128)} %copy.158, f32[16,3,32,256]{2,1,3,0:T(4,128)} %copy.157), kind=kOutput, calls=%fused_computation.225 | convolution fusion | flops 14155776 | bytes 3293184 | tf_op jit(solution)/shard_map/pwakf,pwbkf->pabf/dot_general | solution.py:99
  94.8 29.9 %subtract_bitcast_fusion.2 = f32[16,3,3,256]{1,2,3,0:T(4,128)} fusion(f32[16,256,3,3]{3,2,1,0:T(4,128)S(1)} %fusion.150, f32[16,3,32,256]{2,1,3,0:T(4,128)S(1)} %copy-done.1, f32[16,3,32,256]{2,1,3,0:T(4,128)S(1)} %copy-done), kind=kOutput, calls=%fused_computation.9 | convolution fusion | flops 14192640 | bytes 3440640 | tf_op jit(solution)/shard_map/pwakf,pwbkf->pabf/dot_general | solution.py:99
  124.7 4.9 copy.163
  129.6 6.1 copy.164
  135.7 30.4 %fusion.149 = f32[16,256,3,3]{3,2,1,0:T(4,128)S(1)} fusion(f32[16,3,32,256]{2,1,3,0:T(4,128)} %copy.164, f32[16,3,32,256]{2,1,3,0:T(4,128)} %copy.155), kind=kOutput, calls=%fused_computation.224 | convolution fusion | flops 14155776 | bytes 3293184 | tf_op jit(solution)/shard_map/pwakf,pwbkf->pabf/dot_general | solution.py:99
  166.2 31.9 %add_bitcast_fusion.2 = f32[16,3,3,256]{1,2,3,0:T(4,128)} fusion(f32[16,256,3,3]{3,2,1,0:T(4,128)S(1)} %fusion.149, f32[16,3,32,256]{2,1,3,0:T(4,128)} %copy.156, f32[16,3,32,256]{2,1,3,0:T(4,128)} %copy.157), kind=kOutput, calls=%fused_computation.10 | convolution fusion | flops 14192640 | bytes 3440640 | tf_op jit(solution)/shard_map/pwakf,pwbkf->pabf/dot_general | solution.py:99
  198.1 5.0 copy.162
  203.5 10.3 %all-gather = f32[64,3,3,256]{3,0,2,1:T(8,128)S(1)} all-gather(f32[16,3,3,256]{3,0,2,1:T(8,128)S(1)} %fusion.47), channel_id=2, replica_groups=mesh['stn'=8,'win'=4] {'win'}, dimensions={0}, use_global_device_ids=true | all-gather | bytes 737280 | tf_op jit(solution)/shard_map/all_gather | solution.py:11
  214.6 5.1 copy.174
  219.7 37.0 %fusion.151 = f32[16,256,32,3]{2,3,1,0:T(4,128)} fusion(f32[16,3,32,256]{2,1,3,0:T(4,128)} %copy.164, f32[16,3,3,256]{1,2,3,0:T(4,128)} %copy.174), kind=kOutput, calls=%fused_computation.226 | convolution fusion | flops 14155776 | bytes 3293184 | tf_op jit(solution)/shard_map/pabf,pwbkf->pwakf/dot_general | solution.py:122
  256.7 30.2 %fusion.153 = f32[16,256,3,32]{3,2,1,0:T(4,128)} fusion(f32[16,3,3,256]{1,2,3,0:T(4,128)S(1)} %copy-done.3, f32[16,3,32,256]{2,1,3,0:T(4,128)} %copy.155), kind=kOutput, calls=%fused_computation.228 | convolution fusion | flops 14155776 | bytes 3293184 | tf_op jit(solution)/shard_map/pwakf,pabf->pwbkf/dot_general | solution.py:130
  286.9 4.8 copy.169
  291.7 32.2 %fusion.152 = f32[16,256,32,3]{2,3,1,0:T(4,128)} fusion(f32[16,3,32,256]{2,1,3,0:T(4,128)} %copy.158, f32[16,3,3,256]{2,1,3,0:T(4,128)} %copy.169), kind=kOutput, calls=%fused_computation.227 | convolution fusion | flops 14155776 | bytes 3293184 | tf_op jit(solution)/shard_map/pabf,pwbkf->pwakf/dot_general | solution.py:122
  323.9 4.8 copy.166
  338.0 31.0 %fusion.154 = f32[16,256,3,32]{3,2,1,0:T(4,128)} fusion(f32[16,3,3,256]{1,2,3,0:T(4,128)} %copy.176, f32[16,3,32,256]{2,1,3,0:T(4,128)} %copy.155), kind=kOutput, calls=%fused_computation.229 | convolution fusion | flops 14155776 | bytes 3293184 | tf_op jit(solution)/shard_map/pwakf,pabf->pwbkf/dot_general | solution.py:130
  369.0 30.8 %fusion.155 = f32[16,256,3,32]{3,2,1,0:T(4,128)} fusion(f32[16,3,3,256]{1,2,3,0:T(4,128)S(1)} %copy-done.2, f32[16,3,32,256]{2,1,3,0:T(4,128)} %copy.157), kind=kOutput, calls=%fused_computation.230 | convolution fusion | flops 14155776 | bytes 3293184 | tf_op jit(solution)/shard_map/pwakf,pabf->pwbkf/dot_general | solution.py:130
  399.9 36.7 %subtract_bitcast_fusion.1 = f32[16,1,3,32,256]{3,2,4,0,1:T(4,128)} fusion(f32[16,256,32,3]{2,3,1,0:T(4,128)} %fusion.152, f32[16,3,32,256]{2,1,3,0:T(4,128)S(1)} %bitcast.170, f32[16,3,3,256]{1,2,3,0:T(4,128)S(1)} %copy-done.2), kind=kOutput, calls=%fused_computation.7 | convolution fusion | flops 14548992 | bytes 4866048 | tf_op jit(solution)/shard_map/pabf,pwbkf->pwakf/dot_general | solution.py:122
  436.6 36.0 %add_bitcast_fusion.1 = f32[16,1,3,32,256]{3,2,4,0,1:T(4,128)} fusion(f32[16,256,32,3]{2,3,1,0:T(4,128)S(1)} %bitcast.172, f32[16,3,32,256]{2,1,3,0:T(4,128)S(1)} %bitcast.170, f32[16,3,3,256]{1,2,3,0:T(4,128)S(1)} %bitcast.168), kind=kOutput, calls=%fused_computation.8 | convolution fusion | flops 14548992 | bytes 4866048 | tf_op jit(solution)/shard_map/pabf,pwbkf->pwakf/dot_general | solution.py:122
  472.6 11.9 %maximum_bitcast_fusion = f32[16,3,32,512]{2,1,3,0:T(4,128)} fusion(f32[16,1,3,32,256]{3,2,4,0,1:T(4,128)S(1)} %copy-done.5, f32[16,1,3,32,256]{3,2,4,0,1:T(4,128)} %add_bitcast_fusion.1), kind=kLoop, calls=%fused_computation.1 | loop fusion | flops 786432 | bytes 6291456 | tf_op jit(solution)/shard_map/reshape.43
  484.5 9.5 %copy.172 = f32[16,3,32,512]{3,0,2,1:T(8,128)S(1)} copy(f32[16,3,32,512]{2,1,3,0:T(4,128)} %maximum_bitcast_fusion) | data formatting | bytes 6291456 | tf_op jit(solution)/shard_map/reshape.43
  504.6 31.8 %subtract_bitcast_fusion = f32[16,1,3,32,256]{3,2,4,0,1:T(4,128)} fusion(f32[16,256,3,32]{3,2,1,0:T(4,128)} %fusion.153, f32[16,3,3,256]{1,2,3,0:T(4,128)} %copy.176, f32[16,3,32,256]{2,1,3,0:T(4,128)} %copy.157), kind=kOutput, calls=%fused_computation.6 | convolution fusion | flops 14548992 | bytes 4866048 | tf_op jit(solution)/shard_map/pwakf,pabf->pwbkf/dot_general | solution.py:130
  536.4 31.8 %add_bitcast_fusion = f32[16,1,3,32,256]{3,2,4,0,1:T(4,128)} fusion(f32[16,256,3,32]{3,2,1,0:T(4,128)} %fusion.154, f32[16,256,3,32]{3,2,1,0:T(4,128)} %fusion.155, f32[16,3,3,256]{1,2,3,0:T(4,128)S(1)} %copy-done.4, f32[16,3,32,256]{2,1,3,0:T(4,128)} %copy.157), kind=kOutput, calls=%fused_computation.5 | convolution fusion | flops 14942208 | bytes 6438912 | tf_op jit(solution)/shard_map/pwakf,pabf->pwbkf/dot_general | solution.py:130
  568.3 15.0 %maximum_bitcast_fusion.1 = f32[16,3,32,512]{2,1,3,0:T(4,128)} fusion(f32[16,1,3,32,256]{3,2,4,0,1:T(4,128)} %add_bitcast_fusion, f32[16,1,3,32,256]{3,2,4,0,1:T(4,128)} %subtract_bitcast_fusion), kind=kLoop, calls=%fused_computation.2 | loop fusion | flops 786432 | bytes 6291456 | tf_op jit(solution)/shard_map/reshape.57
  583.2 9.8 %copy.184 = f32[16,3,32,512]{3,0,2,1:T(8,128)S(1)} copy(f32[16,3,32,512]{2,1,3,0:T(4,128)} %maximum_bitcast_fusion.1) | data formatting | bytes 6291456 | tf_op jit(solution)/shard_map/reshape.57
  608.1 13.8 %all-to-all-done.1 = bf16[8,1,1,3,8192]{4,3,2,1,0:T(4,128)(2,1)S(1)} async-done(((bf16[8,1,1,3,8192]{4,3,2,1,0:T(4,128)(2,1)}), bf16[8,1,1,3,8192]{4,3,2,1,0:T(4,128)(2,1)S(1)}, u32[]{:S(2)}, u32[]{:S(2)}) %all-to-all-start.1) | async-done | bytes 393248 | tf_op jit(solution)/shard_map/all_to_all | solution.py:155
  (118 shorter events, 57.7 us)
Async XLA Ops:
  2.0 27.6 %copy-start.22 = (s32[16]{0:T(128)S(1)}, s32[16]{0:T(128)}, u32[]{:S(2)}) copy-start(s32[16]{0:T(128)} %param.13) | copy-start | bytes 196
  5.9 21.7 %all-to-all-start = ((bf16[8,1,1,3,8192]{4,3,2,1,0:T(4,128)(2,1)}), bf16[8,1,1,3,8192]{4,3,2,1,0:T(4,128)(2,1)S(1)}, u32[]{:S(2)}, u32[]{:S(2)}) async-start(bf16[8,1,1,3,8192]{4,3,2,1,0:T(4,128)(2,1)} %fusion.46), calls=%async_computation | async-start | bytes 1048576 | tf_op jit(solution)/shard_map/all_to_all | solution.py:59
  12.3 19.4 %copy-start.17 = (f32[256]{0:T(256)}, f32[256]{0:T(256)S(1)}, u32[]{:S(2)}) copy-start(f32[256]{0:T(256)S(1)} %broadcast_subtract_fusion) | copy-start | bytes 3076
  12.3 19.4 %copy-start.19 = (f32[256]{0:T(256)}, f32[256]{0:T(256)S(1)}, u32[]{:S(2)}) copy-start(f32[256]{0:T(256)S(1)} %fusion.138) | copy-start | bytes 3076
  34.6 7.6 %copy-start.21 = (s32[16]{0:T(128)S(1)}, s32[16]{0:T(128)}, u32[]{:S(2)}) copy-start(s32[16]{0:T(128)} %param.12) | copy-start | bytes 196
  64.4 30.5 %copy-start = (f32[16,3,32,256]{2,1,3,0:T(4,128)S(1)}, f32[16,3,32,256]{2,1,3,0:T(4,128)}, u32[]{:S(2)}) copy-start(f32[16,3,32,256]{2,1,3,0:T(4,128)} %copy.155) | copy-start | bytes 4718596
  64.4 30.5 %copy-start.1 = (f32[16,3,32,256]{2,1,3,0:T(4,128)S(1)}, f32[16,3,32,256]{2,1,3,0:T(4,128)}, u32[]{:S(2)}) copy-start(f32[16,3,32,256]{2,1,3,0:T(4,128)} %copy.156) | copy-start | bytes 4718596
  198.1 5.0 copy-start.7
  198.1 5.0 copy-start.9
  198.1 15.8 %copy-start.16 = (f32[16,3,3,256]{3,0,2,1:T(8,128)S(1)}, f32[16,3,3,256]{3,0,2,1:T(8,128)}, u32[]{:S(2)}) copy-start(f32[16,3,3,256]{3,0,2,1:T(8,128)} %param.8) | copy-start | bytes 442372
  198.1 16.2 %copy-start.18 = (f32[256]{0:T(256)S(1)}, f32[256]{0:T(256)}, u32[]{:S(2)}) copy-start(f32[256]{0:T(256)} %copy-done.17) | copy-start | bytes 3076
  198.1 16.2 %copy-start.20 = (f32[256]{0:T(256)S(1)}, f32[256]{0:T(256)}, u32[]{:S(2)}) copy-start(f32[256]{0:T(256)} %copy-done.19) | copy-start | bytes 3076
  219.7 37.0 %copy-start.3 = (f32[16,3,3,256]{1,2,3,0:T(4,128)S(1)}, f32[16,3,3,256]{1,2,3,0:T(4,128)}, u32[]{:S(2)}) copy-start(f32[16,3,3,256]{1,2,3,0:T(4,128)} %copy.174) | copy-start | bytes 442372
  338.0 31.0 %copy-start.2 = (f32[16,3,3,256]{1,2,3,0:T(4,128)S(1)}, f32[16,3,3,256]{1,2,3,0:T(4,128)}, u32[]{:S(2)}) copy-start(f32[16,3,3,256]{1,2,3,0:T(4,128)} %copy.180) | copy-start | bytes 442372
  338.0 61.9 %slice-start.2 = ((s8[8388608]{0:T(1024)(128)(4,1)}), s8[4194304]{0:T(1024)(128)(4,1)S(1)}, s32[]{:S(2)}) async-start(s8[8388608]{0:T(1024)(128)(4,1)} %bitcast.169), calls=%async_computation.4 | async-start | bytes 8388608
  369.0 30.9 %slice-start.3 = ((s8[8388608]{0:T(1024)(128)(4,1)}), s8[4194304]{0:T(1024)(128)(4,1)S(1)}, s32[]{:S(2)}) async-start(s8[8388608]{0:T(1024)(128)(4,1)} %bitcast.169), calls=%async_computation.5 | async-start | bytes 8388608
  369.0 67.5 %slice-start = ((s8[8388608]{0:T(1024)(128)(4,1)}), s8[4194304]{0:T(1024)(128)(4,1)S(1)}, s32[]{:S(2)}) async-start(s8[8388608]{0:T(1024)(128)(4,1)} %bitcast.167), calls=%async_computation.2 | async-start | bytes 8388608
  369.0 67.5 %slice-start.4 = ((s8[8388608]{0:T(1024)(128)(4,1)}), s8[4194304]{0:T(1024)(128)(4,1)S(1)}, s32[]{:S(2)}) async-start(s8[8388608]{0:T(1024)(128)(4,1)} %bitcast.171), calls=%async_computation.6 | async-start | bytes 8388608
  399.9 36.7 %slice-start.1 = ((s8[8388608]{0:T(1024)(128)(4,1)}), s8[4194304]{0:T(1024)(128)(4,1)S(1)}, s32[]{:S(2)}) async-start(s8[8388608]{0:T(1024)(128)(4,1)} %bitcast.167), calls=%async_computation.3 | async-start | bytes 8388608
  399.9 36.7 %slice-start.5 = ((s8[8388608]{0:T(1024)(128)(4,1)}), s8[4194304]{0:T(1024)(128)(4,1)S(1)}, s32[]{:S(2)}) async-start(s8[8388608]{0:T(1024)(128)(4,1)} %bitcast.171), calls=%async_computation.7 | async-start | bytes 8388608
  436.6 36.0 %copy-start.5 = (f32[16,1,3,32,256]{3,2,4,0,1:T(4,128)S(1)}, f32[16,1,3,32,256]{3,2,4,0,1:T(4,128)}, u32[]{:S(2)}) copy-start(f32[16,1,3,32,256]{3,2,4,0,1:T(4,128)} %subtract_bitcast_fusion.1) | copy-start | bytes 4718596
  484.5 11.4 %copy-start.8 = (f32[256,256]{1,0:T(8,128)S(1)}, f32[256,256]{1,0:T(8,128)}, u32[]{:S(2)}) copy-start(f32[256,256]{1,0:T(8,128)} %get-tuple-element.19) | copy-start | bytes 786436
  504.6 31.8 %copy-start.4 = (f32[16,3,3,256]{1,2,3,0:T(4,128)S(1)}, f32[16,3,3,256]{1,2,3,0:T(4,128)}, u32[]{:S(2)}) copy-start(f32[16,3,3,256]{1,2,3,0:T(4,128)} %copy.182) | copy-start | bytes 442372
  583.2 9.8 %copy-start.23 = (s32[16]{0:T(128)S(1)}, s32[16]{0:T(128)}, u32[]{:S(2)}) copy-start(s32[16]{0:T(128)} %param.13) | copy-start | bytes 196
  583.2 11.1 %copy-start.14 = (f32[256,256]{1,0:T(8,128)S(1)}, f32[256,256]{1,0:T(8,128)}, u32[]{:S(2)}) copy-start(f32[256,256]{1,0:T(8,128)} %get-tuple-element.17) | copy-start | bytes 786436
  583.2 11.1 %copy-start.25 = (f32[256]{0:T(256)S(1)}, f32[256]{0:T(256)}, u32[]{:S(2)}) copy-start(f32[256]{0:T(256)} %compare_convert_fusion) | copy-start | bytes 3076
  593.0 4.5 copy-start.12
  593.0 6.7 %copy-start.6 = (f32[8,3,32,256]{3,2,1,0:T(8,128)S(1)}, f32[8,3,32,256]{3,2,1,0:T(8,128)}, u32[]{:S(2)}) copy-start(f32[8,3,32,256]{3,2,1,0:T(8,128)} %fusion.3) | copy-start | bytes 2359300
  593.0 6.7 %copy-start.10 = (f32[256,256]{1,0:T(8,128)S(1)}, f32[256,256]{1,0:T(8,128)}, u32[]{:S(2)}) copy-start(f32[256,256]{1,0:T(8,128)} %get-tuple-element.13) | copy-start | bytes 786436
  593.1 6.7 %copy-start.11 = (f32[256,256]{1,0:T(8,128)S(1)}, f32[256,256]{1,0:T(8,128)}, u32[]{:S(2)}) copy-start(f32[256,256]{1,0:T(8,128)} %get-tuple-element.14) | copy-start | bytes 786436
  593.1 28.8 %copy-start.26 = (s32[1,8,1]{1,2,0:T(1,128)S(1)}, s32[1,8,1]{1,2,0:T(1,128)}, u32[]{:S(2)}) copy-start(s32[1,8,1]{1,2,0:T(1,128)} %param.11) | copy-start | bytes 100
  603.0 18.8 %all-to-all-start.1 = ((bf16[8,1,1,3,8192]{4,3,2,1,0:T(4,128)(2,1)}), bf16[8,1,1,3,8192]{4,3,2,1,0:T(4,128)(2,1)S(1)}, u32[]{:S(2)}, u32[]{:S(2)}) async-start(bf16[8,1,1,3,8192]{4,3,2,1,0:T(4,128)(2,1)} %bitcast.62), calls=%async_computation.1 | async-start | bytes 1048576 | tf_op jit(solution)/shard_map/all_to_all | solution.py:155
  (3 other events, 9.7 us)
